TPU v7x, 256 devices: a whole 4x4x8 slice. The times are simulated.
256 devices in a mesh: mem: 16 (over z, core), lat: 16 (over y, x).
Axes of the slice: x: 4, y: 4, z: 8, core: 2. Of those that a mesh axis runs over, the one named last changes fastest.
Arguments:
- state: bfloat16 [64, 12, 256, 2048], P('mem', None, 'lat'), may hold values from -6 to 6
- obs_cell: int32 [16, 16, 16384], P('lat', 'mem'), may hold values from 0 to 2047
- obs_value: float32 [16, 16, 16384], P('lat', 'mem'), may hold values from -6 to 6
- obs_rinv: float32 [16, 16, 16384], P('lat', 'mem'), may hold values from 0.005 to 0.1
- obs_count: int32 [16, 16], P('lat', 'mem'), may hold values from 1 to 16384, as said below
- loc_blocks: int32 [16, 16, 9], P('lat', 'mem'), may hold values 0 or 1
- chan_weight: float32 [12], replicated, may hold values from -1.75 to 1.75
Outputs:
- analysis: bfloat16 [64, 12, 256, 2048], P('mem', None, 'lat')
Inputs may be any that keep to these rules, and one draw needn't show every extreme that they name: `obs_count`: some region has exactly 16384 live slots.
All inputs are finite; a program needn't handle non-finite values. No bound on the sum of `loc_blocks` on one device may be relied on, other than what follows from the above.
Results may differ from a plain program's by a relative error of at most 0.007.
Values may be sent and summed in bfloat16 or wider, within the bound.
A program may use at most 64 MiB of HBM per device.

v0:
```python
import jax
import jax.numpy as jnp
from jax import lax
from jax.sharding import PartitionSpec as P

NS_ITERS = 5


def padded(value, sides, width, wrap):
    for axis, dim in sides:
        peers, length = (lax.axis_size(axis), value.shape[dim])
        up = [(i, (i + 1) % peers) for i in range(peers if wrap else peers - 1)]
        down = [(j, i) for i, j in up]
        last = lax.slice_in_dim(value, length - width, length, axis=dim)
        initial = lax.slice_in_dim(value, 0, width, axis=dim)
        before = lax.ppermute(last, axis, up)
        after = lax.ppermute(initial, axis, down)
        value = jnp.concatenate([before, value, after], axis=dim)
    return value


def inverse_root(matrix):
    size_k = matrix.shape[-1]
    identity = jnp.eye(size_k, dtype=jnp.float32)
    frobenius = jnp.sqrt(jnp.sum(matrix * matrix, axis=(-2, -1), keepdims=True))
    current = matrix / frobenius
    inverse = jnp.broadcast_to(identity, matrix.shape)
    for sweep_index in range(NS_ITERS):
        middle = 0.5 * (
            3.0 * identity - jnp.matmul(inverse, current, precision=lax.Precision.HIGHEST)
        )
        current = jnp.matmul(current, middle, precision=lax.Precision.HIGHEST)
        inverse = jnp.matmul(middle, inverse, precision=lax.Precision.HIGHEST)
    return inverse / jnp.sqrt(frobenius)


def weights_from(combined):
    members = combined.shape[-1] - 1
    gram_part = combined[:, :members, :members]
    across = combined[:, :members, members]
    system = (members - 1.0) * jnp.eye(members, dtype=jnp.float32) + gram_part
    root_matrix = inverse_root(system)
    half_step = jnp.einsum("rjk,rk->rj", root_matrix, across, precision=lax.Precision.HIGHEST)
    shift_mean = jnp.einsum("rjk,rk->rj", root_matrix, half_step, precision=lax.Precision.HIGHEST)
    return (jnp.sqrt(members - 1.0) * root_matrix + shift_mean[:, :, None]).astype(jnp.bfloat16)


def pick_cells(table_high, table_low, cell_ids, block_size):
    cells = table_high.shape[1]
    blocks = cell_ids.shape[0] // block_size
    id_blocks = cell_ids.reshape(blocks, block_size)

    def one_block(block_ids):
        onehot = (
            lax.broadcasted_iota(jnp.int32, (cells, block_size), 0) == block_ids[None, :]
        ).astype(jnp.bfloat16)
        high_part = jnp.dot(table_high, onehot, preferred_element_type=jnp.float32)
        return high_part + jnp.dot(table_low, onehot, preferred_element_type=jnp.float32)

    picked = lax.map(one_block, id_blocks)
    return jnp.moveaxis(picked, 0, 1).reshape(table_high.shape[0], blocks * block_size)


def shards(state, obs_cell, obs_value, obs_rinv, obs_count, loc_blocks, chan_weight):
    members_dev, channels, band_rows, full_width = state.shape
    groups = lax.axis_size("mem")
    grouped = state.reshape(members_dev, channels, band_rows, groups, full_width // groups)
    arrived = lax.all_to_all(grouped, "mem", split_axis=3, concat_axis=0, tiled=True)
    members = arrived.shape[0]
    local_width = arrived.shape[4]
    regional = arrived.reshape(members, channels, band_rows, local_width)
    regions = obs_cell.shape[1]
    capacity = obs_cell.shape[2]
    reg_width = local_width // regions
    block_size = min(capacity, 2048)
    projected = regional[:, 0].astype(jnp.float32) * chan_weight[0]
    for channel in range(1, channels):
        projected = projected + regional[:, channel].astype(jnp.float32) * chan_weight[channel]
    table = projected.reshape(members, band_rows, regions, reg_width).transpose(2, 0, 1, 3)
    table = table.reshape(regions, members, band_rows * reg_width)
    table_high = table.astype(jnp.bfloat16)
    table_low = (table - table_high.astype(jnp.float32)).astype(jnp.bfloat16)
    region = 0
    value_list = [
        pick_cells(table_high[region], table_low[region], obs_cell[0, region], block_size)
    ]
    values_at = jnp.stack(value_list)
    obs_mean = jnp.mean(values_at, axis=1, keepdims=True)
    live_slots = (jnp.arange(capacity)[None, :] < obs_count[0][:, None]).astype(jnp.float32)
    obs_scale = jnp.sqrt(obs_rinv[0]) * live_slots
    obs_pert = (values_at - obs_mean) * obs_scale[:, None, :]
    innovation = (obs_value[0] - obs_mean[:, 0, :]) * obs_scale
    slot_rows = jnp.concatenate([obs_pert, innovation[:, None, :]], 1).astype(jnp.bfloat16)
    own_gram = jnp.einsum("rkn,rln->rkl", slot_rows, slot_rows, preferred_element_type=jnp.float32)[
        None
    ]
    wide_lon = padded(own_gram, (("mem", 1),), 1, True)
    nearby = padded(wide_lon.astype(jnp.bfloat16), (("lat", 0),), 1, False).astype(wide_lon.dtype)
    factors = loc_blocks[0].astype(jnp.float32)
    combined = jnp.zeros((regions, members + 1, members + 1), jnp.float32)
    for row_off in range(3):
        for col_off in range(3):
            factor = factors[:, 3 * row_off + col_off][:, None, None]
            combined = combined + factor * nearby[row_off, col_off : col_off + regions]
    transforms = weights_from(combined)
    mean_state = jnp.mean(regional, axis=0, dtype=jnp.float32)
    perts = (regional.astype(jnp.float32) - mean_state).astype(jnp.bfloat16)
    region = 0
    part_perts = perts.reshape(members, -1)
    part_mean = mean_state.reshape(1, -1)
    shifted = lax.dot_general(
        transforms[region], part_perts, (((0,), (0,)), ((), ())), preferred_element_type=jnp.float32
    )
    piece = (part_mean + shifted).astype(jnp.bfloat16)
    pieces = piece.reshape(members, channels, band_rows, reg_width)
    analysis = pieces.reshape(members, channels, band_rows, 1, local_width)
    returned = lax.all_to_all(analysis, "mem", split_axis=0, concat_axis=3, tiled=True)
    return returned.reshape(members_dev, channels, band_rows, full_width)


def solution(mesh):
    placed = (
        P("mem", None, "lat", None),
        P("lat", "mem", None),
        P("lat", "mem", None),
        P("lat", "mem", None),
        P("lat", "mem"),
        P("lat", "mem", None),
        P(),
    )
    return jax.shard_map(
        shards, mesh=mesh, in_specs=placed, out_specs=P("mem", None, "lat", None), check_vma=False
    )
```

profile of v0, /device:TPU:9, one launch (start us, length us, event | category | flops | bytes accessed | tf_op | source)
XLA Modules:
  0.0 294.2 jit_solution(13832654710389450216)
XLA Ops:
  0.0 1.9 copy-done
  1.9 2.6 copy_bitcast_fusion
  4.5 9.3 %all-to-all-start = ((bf16[4,12,16,16,128]{4,2,1,0,3:T(8,128)(2,1)}), bf16[4,12,16,16,128]{4,2,1,0,3:T(8,128)(2,1)}, u32[]{:S(2)}, u32[]{:S(2)}) async-start(bf16[4,12,16,16,128]{4,2,1,0,3:T(8,128)(2,1)} %copy_bitcast_fusion), calls=%async_computation | async-start | bytes 6291456 | tf_op jit(solution)/shard_map/all_to_all | solution.py:68
  13.7 0.5 broadcast.361
  14.3 0.8 reduce.7
  15.7 0.7 fusion.48
  16.4 0.7 fusion.49
  17.1 67.7 %all-to-all-done = bf16[4,12,16,16,128]{4,2,1,0,3:T(8,128)(2,1)} async-done(((bf16[4,12,16,16,128]{4,2,1,0,3:T(8,128)(2,1)}), bf16[4,12,16,16,128]{4,2,1,0,3:T(8,128)(2,1)}, u32[]{:S(2)}, u32[]{:S(2)}) %all-to-all-start) | async-done | bytes 3145760 | tf_op jit(solution)/shard_map/all_to_all | solution.py:68
  84.8 9.9 %add_add_fusion = f32[64,1,16,128]{3,2,0,1:T(8,128)S(1)} fusion(bf16[64,12,16,128]{3,2,1,0:T(8,128)(2,1)} %bitcast.9, f32[]{:T(128)} %bitcast.22, f32[]{:T(128)} %bitcast.21, f32[]{:T(128)} %bitcast.20, f32[]{:T(128)} %bitcast.19, f32[]{:T(128)} %bitcast.18, f32[]{:T(128)} %bitcast.17, f32[]{:T(128)} %bitcast.16, f32[]{:T(128)} %bitcast.15, f32[]{:T(128)} %bitcast.14, ...), kind=kLoop, calls=%fused_computation.39 | loop fusion | flops 4587520 | bytes 3670064 | tf_op jit(solution)/shard_map/add | solution.py:78
  94.8 0.2 copy.63
  94.9 0.9 fusion.22
  95.8 61.0 %while.10 = (s32[]{:T(128)}, f32[8,64,2048]{2,1,0:T(8,128)}, s32[8,2048]{1,0:T(8,128)S(1)}, bf16[64,2048]{1,0:T(8,128)(2,1)S(1)}, bf16[64,2048]{1,0:T(8,128)(2,1)}, /*index=5*/s32[]{:T(128)}) while((s32[]{:T(128)}, f32[8,64,2048]{2,1,0:T(8,128)}, s32[8,2048]{1,0:T(8,128)S(1)}, bf16[64,2048]{1,0:T(8,128)(2,1)S(1)}, bf16[64,2048]{1,0:T(8,128)(2,1)}, ...), condition=%wide.region_2.3_spmd, body=%wide.region_1.2_spmd.sunk | while | flops 1082261504 | bytes 2130505 | solution.py:60
  95.8 3.9 %fusion.93 = f32[2048,64]{0,1:T(8,128)S(1)} fusion(bf16[64,2048]{1,0:T(8,128)(2,1)} %get-tuple-element.115, s32[2048]{0:T(1024)S(1)} %bitcast.198), kind=kOutput, calls=%fused_computation.1.clone.1 | convolution fusion | flops 541065216 | bytes 794624 | tf_op jit(solution)/shard_map/while/body/eval_jaxpr/dot_general | solution.py:58
  99.7 3.7 %fusion.94 = f32[8,64,2048]{2,1,0:T(8,128)} fusion(f32[8,64,2048]{2,1,0:T(8,128)} %get-tuple-element.106, s32[]{:T(128)} %get-tuple-element.105, f32[2048,64]{0,1:T(8,128)S(1)} %fusion.93, bf16[64,2048]{1,0:T(8,128)(2,1)S(1)} %get-tuple-element.114, s32[2048]{0:T(1024)S(1)} %bitcast.199), kind=kOutput, calls=%fused_computation.7.clone.1 | convolution fusion | flops 541196288 | bytes 1319424 | tf_op jit(solution)/shard_map/while/body/eval_jaxpr/dot_general | solution.py:57
  103.4 3.9 %fusion.93 = f32[2048,64]{0,1:T(8,128)S(1)} fusion(bf16[64,2048]{1,0:T(8,128)(2,1)} %get-tuple-element.115, s32[2048]{0:T(1024)S(1)} %bitcast.198), kind=kOutput, calls=%fused_computation.1.clone.1 | convolution fusion | flops 541065216 | bytes 794624 | tf_op jit(solution)/shard_map/while/body/eval_jaxpr/dot_general | solution.py:58
  107.3 3.7 %fusion.94 = f32[8,64,2048]{2,1,0:T(8,128)} fusion(f32[8,64,2048]{2,1,0:T(8,128)} %get-tuple-element.106, s32[]{:T(128)} %get-tuple-element.105, f32[2048,64]{0,1:T(8,128)S(1)} %fusion.93, bf16[64,2048]{1,0:T(8,128)(2,1)S(1)} %get-tuple-element.114, s32[2048]{0:T(1024)S(1)} %bitcast.199), kind=kOutput, calls=%fused_computation.7.clone.1 | convolution fusion | flops 541196288 | bytes 1319424 | tf_op jit(solution)/shard_map/while/body/eval_jaxpr/dot_general | solution.py:57
  111.0 3.9 %fusion.93 = f32[2048,64]{0,1:T(8,128)S(1)} fusion(bf16[64,2048]{1,0:T(8,128)(2,1)} %get-tuple-element.115, s32[2048]{0:T(1024)S(1)} %bitcast.198), kind=kOutput, calls=%fused_computation.1.clone.1 | convolution fusion | flops 541065216 | bytes 794624 | tf_op jit(solution)/shard_map/while/body/eval_jaxpr/dot_general | solution.py:58
  114.9 3.7 %fusion.94 = f32[8,64,2048]{2,1,0:T(8,128)} fusion(f32[8,64,2048]{2,1,0:T(8,128)} %get-tuple-element.106, s32[]{:T(128)} %get-tuple-element.105, f32[2048,64]{0,1:T(8,128)S(1)} %fusion.93, bf16[64,2048]{1,0:T(8,128)(2,1)S(1)} %get-tuple-element.114, s32[2048]{0:T(1024)S(1)} %bitcast.199), kind=kOutput, calls=%fused_computation.7.clone.1 | convolution fusion | flops 541196288 | bytes 1319424 | tf_op jit(solution)/shard_map/while/body/eval_jaxpr/dot_general | solution.py:57
  118.7 3.9 %fusion.93 = f32[2048,64]{0,1:T(8,128)S(1)} fusion(bf16[64,2048]{1,0:T(8,128)(2,1)} %get-tuple-element.115, s32[2048]{0:T(1024)S(1)} %bitcast.198), kind=kOutput, calls=%fused_computation.1.clone.1 | convolution fusion | flops 541065216 | bytes 794624 | tf_op jit(solution)/shard_map/while/body/eval_jaxpr/dot_general | solution.py:58
  122.6 3.7 %fusion.94 = f32[8,64,2048]{2,1,0:T(8,128)} fusion(f32[8,64,2048]{2,1,0:T(8,128)} %get-tuple-element.106, s32[]{:T(128)} %get-tuple-element.105, f32[2048,64]{0,1:T(8,128)S(1)} %fusion.93, bf16[64,2048]{1,0:T(8,128)(2,1)S(1)} %get-tuple-element.114, s32[2048]{0:T(1024)S(1)} %bitcast.199), kind=kOutput, calls=%fused_computation.7.clone.1 | convolution fusion | flops 541196288 | bytes 1319424 | tf_op jit(solution)/shard_map/while/body/eval_jaxpr/dot_general | solution.py:57
  126.3 3.9 %fusion.93 = f32[2048,64]{0,1:T(8,128)S(1)} fusion(bf16[64,2048]{1,0:T(8,128)(2,1)} %get-tuple-element.115, s32[2048]{0:T(1024)S(1)} %bitcast.198), kind=kOutput, calls=%fused_computation.1.clone.1 | convolution fusion | flops 541065216 | bytes 794624 | tf_op jit(solution)/shard_map/while/body/eval_jaxpr/dot_general | solution.py:58
  130.2 3.7 %fusion.94 = f32[8,64,2048]{2,1,0:T(8,128)} fusion(f32[8,64,2048]{2,1,0:T(8,128)} %get-tuple-element.106, s32[]{:T(128)} %get-tuple-element.105, f32[2048,64]{0,1:T(8,128)S(1)} %fusion.93, bf16[64,2048]{1,0:T(8,128)(2,1)S(1)} %get-tuple-element.114, s32[2048]{0:T(1024)S(1)} %bitcast.199), kind=kOutput, calls=%fused_computation.7.clone.1 | convolution fusion | flops 541196288 | bytes 1319424 | tf_op jit(solution)/shard_map/while/body/eval_jaxpr/dot_general | solution.py:57
  133.9 3.9 %fusion.93 = f32[2048,64]{0,1:T(8,128)S(1)} fusion(bf16[64,2048]{1,0:T(8,128)(2,1)} %get-tuple-element.115, s32[2048]{0:T(1024)S(1)} %bitcast.198), kind=kOutput, calls=%fused_computation.1.clone.1 | convolution fusion | flops 541065216 | bytes 794624 | tf_op jit(solution)/shard_map/while/body/eval_jaxpr/dot_general | solution.py:58
  137.8 3.7 %fusion.94 = f32[8,64,2048]{2,1,0:T(8,128)} fusion(f32[8,64,2048]{2,1,0:T(8,128)} %get-tuple-element.106, s32[]{:T(128)} %get-tuple-element.105, f32[2048,64]{0,1:T(8,128)S(1)} %fusion.93, bf16[64,2048]{1,0:T(8,128)(2,1)S(1)} %get-tuple-element.114, s32[2048]{0:T(1024)S(1)} %bitcast.199), kind=kOutput, calls=%fused_computation.7.clone.1 | convolution fusion | flops 541196288 | bytes 1319424 | tf_op jit(solution)/shard_map/while/body/eval_jaxpr/dot_general | solution.py:57
  141.5 3.9 %fusion.93 = f32[2048,64]{0,1:T(8,128)S(1)} fusion(bf16[64,2048]{1,0:T(8,128)(2,1)} %get-tuple-element.115, s32[2048]{0:T(1024)S(1)} %bitcast.198), kind=kOutput, calls=%fused_computation.1.clone.1 | convolution fusion | flops 541065216 | bytes 794624 | tf_op jit(solution)/shard_map/while/body/eval_jaxpr/dot_general | solution.py:58
  145.4 3.7 %fusion.94 = f32[8,64,2048]{2,1,0:T(8,128)} fusion(f32[8,64,2048]{2,1,0:T(8,128)} %get-tuple-element.106, s32[]{:T(128)} %get-tuple-element.105, f32[2048,64]{0,1:T(8,128)S(1)} %fusion.93, bf16[64,2048]{1,0:T(8,128)(2,1)S(1)} %get-tuple-element.114, s32[2048]{0:T(1024)S(1)} %bitcast.199), kind=kOutput, calls=%fused_computation.7.clone.1 | convolution fusion | flops 541196288 | bytes 1319424 | tf_op jit(solution)/shard_map/while/body/eval_jaxpr/dot_general | solution.py:57
  149.2 3.9 %fusion.93 = f32[2048,64]{0,1:T(8,128)S(1)} fusion(bf16[64,2048]{1,0:T(8,128)(2,1)} %get-tuple-element.115, s32[2048]{0:T(1024)S(1)} %bitcast.198), kind=kOutput, calls=%fused_computation.1.clone.1 | convolution fusion | flops 541065216 | bytes 794624 | tf_op jit(solution)/shard_map/while/body/eval_jaxpr/dot_general | solution.py:58
  153.0 3.7 %fusion.94 = f32[8,64,2048]{2,1,0:T(8,128)} fusion(f32[8,64,2048]{2,1,0:T(8,128)} %get-tuple-element.106, s32[]{:T(128)} %get-tuple-element.105, f32[2048,64]{0,1:T(8,128)S(1)} %fusion.93, bf16[64,2048]{1,0:T(8,128)(2,1)S(1)} %get-tuple-element.114, s32[2048]{0:T(1024)S(1)} %bitcast.199), kind=kOutput, calls=%fused_computation.7.clone.1 | convolution fusion | flops 541196288 | bytes 1319424 | tf_op jit(solution)/shard_map/while/body/eval_jaxpr/dot_general | solution.py:57
  156.8 2.6 bitcast_reduce_fusion
  159.4 4.7 %copy.54 = f32[8,8,8,2048]{3,2,0,1:T(8,128)} copy(f32[8,8,8,2048]{3,2,1,0:T(8,128)} %bitcast.63) | data formatting | bytes 8388608 | tf_op jit(solution)/shard_map/stack;reshape | solution.py:87
  164.3 0.2 convert_bitcast_fusion
  164.5 2.6 multiply_convert_fusion
  167.1 0.8 fusion.14
  167.9 0.5 collective-permute-start
  168.4 0.4 collective-permute-start.1
  168.8 2.4 convert_reduce_fusion
  171.2 0.4 collective-permute-done.1
  171.6 3.1 %collective-permute-start.2 = (bf16[1,3,65,65]{2,3,1,0:T(8,128)(2,1)S(1)}, bf16[1,3,65,65]{2,3,1,0:T(8,128)(2,1)S(1)}, u32[]{:S(2)}, u32[]{:S(2)}) collective-permute-start(bf16[1,3,65,65]{2,3,1,0:T(8,128)(2,1)S(1)} %pad_maximum_fusion), channel_id=1, source_target_pairs={{0,1},{1,2},{2,3},{3,4},{4,5},{5,6},{6,7},{7,8},{8,9},{9,10},{10,1... | collective-permute-start | bytes 76058 | tf_op jit(solution)/shard_map/ppermute | solution.py:16
  174.8 4.5 %collective-permute-start.3 = (bf16[1,3,65,65]{2,3,1,0:T(8,128)(2,1)S(1)}, bf16[1,3,65,65]{2,3,1,0:T(8,128)(2,1)S(1)}, u32[]{:S(2)}, u32[]{:S(2)}) collective-permute-start(bf16[1,3,65,65]{2,3,1,0:T(8,128)(2,1)S(1)} %pad_maximum_fusion), channel_id=1, source_target_pairs={{1,0},{2,1},{3,2},{4,3},{5,4},{6,5},{7,6},{8,7},{9,8},{10,9},{11,1... | collective-permute-start | bytes 76058 | tf_op jit(solution)/shard_map/ppermute | solution.py:17
  179.2 4.5 %fusion.8 = bf16[16,4,12,16,1,128]{5,3,2,1,0,4:T(8,128)(2,1)} fusion(bf16[4,12,16,16,128]{4,2,1,0,3:T(8,128)(2,1)} %all-to-all-done, f32[12,16,128]{2,1,0:T(8,128)S(1)} %broadcast_multiply_fusion), kind=kLoop, calls=%fused_computation.13 | loop fusion | flops 4718592 | bytes 6389760 | tf_op jit(solution)/shard_map/convert_element_type | solution.py:107
  183.8 4.8 %convert_element_type.241 = bf16[64,24576]{1,0:T(8,128)(2,1)} reshape(bf16[16,4,12,16,1,128]{5,3,2,1,0,4:T(8,128)(2,1)} %fusion.8) | data formatting | bytes 6291456 | tf_op jit(solution)/shard_map/convert_element_type | solution.py:107
  188.6 5.7 %fusion.24 = f32[1,65,65]{1,2,0:T(8,128)S(1)} fusion(f32[3,3,65,65]{2,3,1,0:T(8,128)S(1)} %maximum_convert_fusion, f32[]{:T(128)} %bitcast.35, f32[]{:T(128)} %bitcast.34, f32[]{:T(128)} %bitcast.33, f32[]{:T(128)} %bitcast.32, f32[]{:T(128)} %bitcast.31, f32[]{:T(128)} %bitcast.30, f32[]{:T(128)} %bitcast.29, f32[]{:T(128)} %bitcast.28, f32[]{:T(128)} %bitcast.7), kind=kLoop, calls=%fused_computation.59 | loop fusion | flops 71825 | bytes 169036 | tf_op jit(solution)/shard_map/add | solution.py:104
  194.2 0.6 multiply_reduce_fusion
  195.5 0.2 fusion.21
  195.7 0.2 fusion.32
  196.0 0.1 fusion.35
  196.1 0.2 fusion.20
  196.3 0.2 fusion.51
  196.5 0.2 fusion.50
  196.6 0.2 fusion.19
  196.8 0.2 fusion.53
  197.0 0.2 fusion.52
  197.1 0.2 fusion.18
  197.3 0.2 fusion.55
  197.5 0.2 fusion.54
  197.7 0.2 fusion.17
  197.9 0.2 convolution_divide_fusion
  198.0 0.1 convolution_bitcast_fusion.1
  198.2 0.2 convolution_bitcast_fusion
  198.4 3.0 %fusion.13 = bf16[8,8,192,128]{3,1,2,0:T(8,128)(2,1)S(1)} fusion(bf16[64,24576]{1,0:T(8,128)(2,1)} %convert_element_type.241, f32[24576]{0:T(1024)S(1)} %bitcast.194, f32[64,64]{1,0:T(8,128)S(1)} %convolution_divide_fusion, f32[64]{0:T(128)S(1)} %convolution_bitcast_fusion), kind=kOutput, calls=%fused_computation.21 | convolution fusion | flops 204484608 | bytes 6406400 | tf_op jit(solution)/shard_map/dot_general | solution.py:111
  201.4 0.8 copy.57
  202.2 80.9 %all_to_all.30 = bf16[64,12,16,1,128]{4,2,1,3,0:T(8,128)(2,1)S(1)} all-to-all(bf16[64,12,16,1,128]{4,2,1,3,0:T(8,128)(2,1)S(1)} %bitcast.190), channel_id=1, replica_groups=mesh['mem'=16,'lat'=16] {'mem'}, dimensions={0} | all-to-all | bytes 6291456 | tf_op jit(solution)/shard_map/all_to_all | solution.py:117
  283.1 5.3 %copy.40 = bf16[4,12,16,16,1,128]{5,3,2,1,0,4:T(8,128)(2,1)} copy(bf16[4,12,16,16,1,128]{5,2,1,0,3,4:T(8,128)(2,1)S(1)} %bitcast.191) | data formatting | bytes 6291456 | tf_op jit(solution)/shard_map/all_to_all | solution.py:117
  288.4 5.8 %reshape.577 = bf16[4,12,16,2048]{3,2,1,0:T(8,128)(2,1)} reshape(bf16[4,12,16,16,1,128]{5,3,2,1,0,4:T(8,128)(2,1)} %copy.40) | data formatting | bytes 6291456 | tf_op jit(solution)/shard_map/reshape | solution.py:118
  (31 shorter events, 0.3 us)
Async XLA Ops:
  0.0 1.9 copy-start
  4.5 9.8 %copy-start.4 = (s32[1,1,16384]{2,1,0:T(1,128)S(1)}, s32[1,1,16384]{2,1,0:T(1,128)}, u32[]{:S(2)}) copy-start(s32[1,1,16384]{2,1,0:T(1,128)} %param.10) | copy-start | bytes 196612
  4.5 11.3 %copy-start.5 = (s32[1,1,9]{2,1,0:T(1,128)S(1)}, s32[1,1,9]{2,1,0:T(1,128)}, u32[]{:S(2)}) copy-start(s32[1,1,9]{2,1,0:T(1,128)} %param.14) | copy-start | bytes 112
  4.5 12.0 %copy-start.1 = (f32[12]{0:T(128)S(1)}, f32[12]{0:T(128)}, u32[]{:S(2)}) copy-start(f32[12]{0:T(128)} %param.15) | copy-start | bytes 148
  4.5 80.4 %all-to-all-start = ((bf16[4,12,16,16,128]{4,2,1,0,3:T(8,128)(2,1)}), bf16[4,12,16,16,128]{4,2,1,0,3:T(8,128)(2,1)}, u32[]{:S(2)}, u32[]{:S(2)}) async-start(bf16[4,12,16,16,128]{4,2,1,0,3:T(8,128)(2,1)} %copy_bitcast_fusion), calls=%async_computation | async-start | bytes 6291456 | tf_op jit(solution)/shard_map/all_to_all | solution.py:68
  159.4 4.9 %copy-start.2 = (f32[1,1,16384]{2,1,0:T(1,128)S(1)}, f32[1,1,16384]{2,1,0:T(1,128)}, u32[]{:S(2)}) copy-start(f32[1,1,16384]{2,1,0:T(1,128)} %param.11) | copy-start | bytes 196612
  159.4 4.9 %copy-start.3 = (f32[1,1,16384]{2,1,0:T(1,128)S(1)}, f32[1,1,16384]{2,1,0:T(1,128)}, u32[]{:S(2)}) copy-start(f32[1,1,16384]{2,1,0:T(1,128)} %param.12) | copy-start | bytes 196612
  167.9 3.3 %collective-permute-start = (bf16[1,1,65,65]{2,3,1,0:T(8,128)(2,1)S(1)}, bf16[1,1,65,65]{2,3,1,0:T(8,128)(2,1)S(1)}, u32[]{:S(2)}, u32[]{:S(2)}) collective-permute-start(bf16[1,1,65,65]{2,3,1,0:T(8,128)(2,1)S(1)} %fusion.14), channel_id=1, source_target_pairs={{0,16},{16,32},{32,48},{48,64},{64,80},{80,96},{96,112},{112,128},... | collective-permute-start | bytes 25358 | tf_op jit(solution)/shard_map/ppermute | solution.py:16
  168.4 3.2 %collective-permute-start.1 = (bf16[1,1,65,65]{2,3,1,0:T(8,128)(2,1)S(1)}, bf16[1,1,65,65]{2,3,1,0:T(8,128)(2,1)S(1)}, u32[]{:S(2)}, u32[]{:S(2)}) collective-permute-start(bf16[1,1,65,65]{2,3,1,0:T(8,128)(2,1)S(1)} %fusion.14), channel_id=1, source_target_pairs={{16,0},{32,16},{48,32},{64,48},{80,64},{96,80},{112,96},{128,112},... | collective-permute-start | bytes 25358 | tf_op jit(solution)/shard_map/ppermute | solution.py:17
  171.6 16.9 %collective-permute-start.2 = (bf16[1,3,65,65]{2,3,1,0:T(8,128)(2,1)S(1)}, bf16[1,3,65,65]{2,3,1,0:T(8,128)(2,1)S(1)}, u32[]{:S(2)}, u32[]{:S(2)}) collective-permute-start(bf16[1,3,65,65]{2,3,1,0:T(8,128)(2,1)S(1)} %pad_maximum_fusion), channel_id=1, source_target_pairs={{0,1},{1,2},{2,3},{3,4},{4,5},{5,6},{6,7},{7,8},{8,9},{9,10},{10,1... | collective-permute-start | bytes 76058 | tf_op jit(solution)/shard_map/ppermute | solution.py:16
  174.8 13.8 %collective-permute-start.3 = (bf16[1,3,65,65]{2,3,1,0:T(8,128)(2,1)S(1)}, bf16[1,3,65,65]{2,3,1,0:T(8,128)(2,1)S(1)}, u32[]{:S(2)}, u32[]{:S(2)}) collective-permute-start(bf16[1,3,65,65]{2,3,1,0:T(8,128)(2,1)S(1)} %pad_maximum_fusion), channel_id=1, source_target_pairs={{1,0},{2,1},{3,2},{4,3},{5,4},{6,5},{7,6},{8,7},{9,8},{10,9},{11,1... | collective-permute-start | bytes 76058 | tf_op jit(solution)/shard_map/ppermute | solution.py:17
where the time goes:
time: 295 us; the launch traced here: 294 us
  blocking collectives  80.9 us (27%)
  waiting for transfers between devices  68.1 us (23%)
  matrix products  67.3 us (23%)
  other arithmetic  30.2 us (10%)
  local copies, waits for them, and re-layouts  28.1 us (10%)
  starting transfers between devices  17.8 us (6%)
    all_to_all x1, blocking collectives, shards(): lax.all_to_all(analysis, 'mem', split_axis=0, concat_axis=3, tiled=True)  80.9 us
    all_to_all x1, waiting for transfers between devices, shards(): lax.all_to_all(grouped, 'mem', split_axis=3, concat_axis=0, tiled=True)  67.7 us
    dot_general x8, matrix products, one_block(): jnp.dot(table_low, onehot, preferred_element_type=jnp.float32)  31 us
    dot_general x8, matrix products, one_block(): high_part = jnp.dot(table_high, onehot, preferred_element_type=jnp.float32)  29.8 us
    add x1, other arithmetic, shards(): projected + regional[:, channel].astype(jnp.float32) * chan_weight[channel]  9.93 us
    all_to_all x1, starting transfers between devices, shards(): lax.all_to_all(grouped, 'mem', split_axis=3, concat_axis=0, tiled=True)  9.28 us
  transfers between devices with their start and end apart: 5, of which 2 were waited for; matrix products, arithmetic and copies ran while one was open for 5% of the time, Pallas kernels for 0%

commit v1 on v0

v1 whole, which is shorter than its diff:
```python
import functools

import jax
import jax.numpy as jnp
from jax import lax
from jax.experimental import pallas as pl
from jax.experimental.pallas import tpu as pltpu
from jax.sharding import PartitionSpec as P

NS_ITERS = 5
MESH = pl.DeviceIdType.MESH
HIGHEST = lax.Precision.HIGHEST
F32 = jnp.float32
BF16 = jnp.bfloat16


def peer(me, size, index):
    step = jnp.maximum(index - 1, 0)
    distance = step // 4 + 1
    offset = jnp.where((step // 2) % 2 == 0, distance, size // 2 - distance)
    offset = jnp.where(index == 0, 0, offset)
    flip = jnp.where(index == 0, 1, step % 2)
    return ((me // 2 + offset) % (size // 2)) * 2 + (me + flip) % 2


def kernel(
    weight, count, loc,
    x, cell, value, rinv,
    out,
    xv, cellv, valuev, rinvv, proj, projected, table, gram, gram_out, near, arrived, spread, weights, perts, means, analysed,
    load_sem, obs_sem, own_sem, proj_send, proj_recv, gram_send, gram_recv, in_send, in_recv, out_send, out_recv,
):
    n = lax.axis_size("mem")
    bands = lax.axis_size("lat")
    me, band = lax.axis_index("mem"), lax.axis_index("lat")
    per, channels, rows, width = x.shape
    members = per * n
    cols = width // n

    loads = [pltpu.make_async_copy(x.at[m], xv.at[m], load_sem.at[m]) for m in range(per)]
    for load in loads:
        load.start()
    obs_loads = [
        pltpu.make_async_copy(source, target, obs_sem.at[i])
        for i, (source, target) in enumerate(((cell, cellv), (value, valuev), (rinv, rinvv)))
    ]
    for load in obs_loads:
        load.start()

    def columns(q):
        return pl.ds(pl.multiple_of(q * cols, cols), cols)

    neighbours = [(i, j) for i in (-1, 0, 1) for j in (-1, 0, 1) if (i, j) != (0, 0)]

    def neighbour(i, j):
        return {"lat": (band + i + bands) % bands, "mem": (me + j + n) % n}

    barrier = pltpu.get_barrier_semaphore()

    def greet(i, carry):
        pl.semaphore_signal(barrier, inc=1, device_id={"mem": peer(me, n, i)}, device_id_type=MESH)
        return carry

    lax.fori_loop(0, n - 1, greet, 0)
    for i, j in neighbours:
        if i != 0:
            pl.semaphore_signal(barrier, inc=1, device_id=neighbour(i, j), device_id_type=MESH)

    wide = 256
    for m in range(per):
        loads[m].wait()

        def project(b, carry):
            at = pl.ds(pl.multiple_of(b * wide, wide), wide)
            total = xv[m, 0, :, at].astype(F32) * weight[0]
            for c in range(1, channels):
                total = total + xv[m, c, :, at].astype(F32) * weight[c]
            proj[m, :, at] = total.astype(BF16)
            return carry

        lax.fori_loop(0, width // wide, project, 0)

    pl.semaphore_wait(barrier, n - 1 + 6)

    mine = pl.ds(pl.multiple_of(me * per, per), per)

    def send_proj(i, carry):
        q = peer(me, n, i)
        pltpu.make_async_remote_copy(
            src_ref=proj.at[:, :, columns(q)],
            dst_ref=projected.at[mine],
            send_sem=proj_send, recv_sem=proj_recv,
            device_id={"mem": q}, device_id_type=MESH,
        ).start()
        return carry

    lax.fori_loop(0, n - 1, send_proj, 0)

    def send_in(c):
        def one(i, carry):
            q = peer(me, n, i)
            pltpu.make_async_remote_copy(
                src_ref=x.at[:, pl.ds(c, 1), :, columns(q)],
                dst_ref=arrived.at[mine, pl.ds(c, 1)],
                send_sem=in_send.at[c], recv_sem=in_recv.at[c],
                device_id={"mem": q}, device_id_type=MESH,
            ).start()
            return carry

        lax.fori_loop(0, n - 1, one, 0)

    def drain(ref, sem):
        pltpu.make_async_copy(ref, ref, sem).wait()

    others = pl.ds(0, members - per)

    def next_in(c):
        drain(arrived.at[others, pl.ds(c - 2, 1)], in_send.at[c - 2])
        send_in(c)

    own_proj = pltpu.make_async_copy(proj.at[:, :, columns(me)], projected.at[mine], own_sem.at[0])
    own_in = pltpu.make_async_copy(x.at[:, :, :, columns(me)], arrived.at[mine], own_sem.at[1])
    own_proj.start()
    own_in.start()
    send_in(0)
    send_in(1)

    for_member = lax.broadcasted_iota(jnp.int32, (members, members * rows), 0)
    spread[...] = jnp.where(
        for_member == lax.broadcasted_iota(jnp.int32, (members, members * rows), 1) // rows, 1.0, 0.0
    ).astype(BF16)

    for load in obs_loads:
        load.wait()
    block = 8
    lanes = cellv.shape[1]
    row_of = lax.broadcasted_iota(jnp.int32, (rows, block * lanes), 0)
    col_of = lax.broadcasted_iota(jnp.int32, (cols, block * lanes), 0)

    def along(tile):
        return jnp.concatenate([tile[i : i + 1, :] for i in range(block)], axis=1)

    def histogram(b, total):
        at = pl.ds(pl.multiple_of(b * block, block), block)
        slot = (
            b * (block * lanes)
            + lax.broadcasted_iota(jnp.int32, (block, lanes), 0) * lanes
            + lax.broadcasted_iota(jnp.int32, (block, lanes), 1)
        )
        live = jnp.where(slot < count[0, 0], rinvv[at, :], 0.0)
        held = live * valuev[at, :]
        cells = along(cellv[at, :])
        hit = row_of == cells // cols
        parts = []
        for term in (live, held):
            high = term.astype(BF16).astype(F32)
            parts += [high, term - high]
        terms = jnp.concatenate([jnp.where(hit, along(part), 0.0) for part in parts], axis=0).astype(BF16)
        onehot = jnp.where(col_of == cells % cols, 1.0, 0.0).astype(BF16)
        return total + lax.dot_general(terms, onehot, (((1,), (1,)), ((), ())), preferred_element_type=F32)

    sums = lax.fori_loop(0, cellv.shape[0] // block, histogram, jnp.zeros((4 * rows, cols), F32))
    cell_rinv = sums[:rows] + sums[rows : 2 * rows]
    cell_held = sums[2 * rows : 3 * rows] + sums[3 * rows :]
    next_in(2)

    own_proj.wait()
    drain(projected.at[others], proj_recv)
    step = 8
    total = jnp.zeros((rows, cols), F32)
    for k in range(0, members, step):
        total = total + jnp.sum(projected[k : k + step].astype(F32), axis=0)
    obs_mean = total * (1.0 / members)
    seen = cell_rinv > 0.0
    root_rinv = jnp.sqrt(cell_rinv)
    inverse = jnp.where(seen, 1.0 / jnp.where(seen, root_rinv, 1.0), 0.0)
    for k in range(0, members, step):
        table[k : k + step] = (projected[k : k + step].astype(F32) - obs_mean[None]) * root_rinv[None]
    tail = table.shape[0] - members
    table[members:] = jnp.zeros((tail, rows, cols), F32)
    table[members] = (cell_held - cell_rinv * obs_mean) * inverse
    lines = jnp.concatenate([table[:, r, :].astype(BF16) for r in range(rows)], axis=1)
    gram[...] = lax.dot_general(lines[:members], lines, (((1,), (1,)), ((), ())), preferred_element_type=F32)
    gram_out[...] = gram[...].astype(BF16)
    next_in(3)

    for s, (i, j) in enumerate(neighbours):
        pltpu.make_async_remote_copy(
            src_ref=gram_out, dst_ref=near.at[7 - s],
            send_sem=gram_send, recv_sem=gram_recv,
            device_id=neighbour(i, j), device_id_type=MESH,
        ).start()
    next_in(4)
    next_in(5)
    drain(near, gram_recv)
    combined = gram[...] * loc[0, 4].astype(F32)
    for s, (i, j) in enumerate(neighbours):
        factor = loc[0, 3 * (i + 1) + (j + 1)]
        if i == -1:
            factor = jnp.where(band > 0, factor, 0)
        if i == 1:
            factor = jnp.where(band < bands - 1, factor, 0)
        combined = combined + factor.astype(F32) * near[s].astype(F32)

    identity = jnp.where(
        lax.broadcasted_iota(jnp.int32, (members, members), 0)
        == lax.broadcasted_iota(jnp.int32, (members, members), 1),
        1.0, 0.0,
    )

    def times(a, b):
        return jnp.dot(a, b, precision=HIGHEST, preferred_element_type=F32)

    system = (members - 1.0) * identity + combined[:, :members]
    across = combined[:, members : members + 1]
    frobenius = jnp.sqrt(jnp.sum(jnp.sum(system * system, axis=1, keepdims=True), axis=0, keepdims=True))
    current = system / frobenius

    inverse = identity
    for _ in range(NS_ITERS):
        middle = 0.5 * (3.0 * identity - times(inverse, current))
        current, inverse = times(current, middle), times(middle, inverse)
    root = inverse / jnp.sqrt(frobenius)
    half = jnp.sum(root * across, axis=0, keepdims=True)
    half = jnp.sum(identity * half, axis=1, keepdims=True)
    shift = jnp.sum(root * half, axis=0, keepdims=True)
    transform = (float(members - 1) ** 0.5 * root + shift).astype(BF16)
    next_in(6)

    tall = 128
    repeated = jnp.dot(transform, spread[...], preferred_element_type=F32).astype(BF16)

    def expand(b, carry):
        at = lax.broadcasted_iota(jnp.int32, (tall, members), 0) + b * tall
        pick = jnp.where(
            at // rows == lax.broadcasted_iota(jnp.int32, (tall, members), 1), 1.0, 0.0
        ).astype(BF16)
        full = jnp.dot(pick, repeated, preferred_element_type=F32)
        same = (
            lax.broadcasted_iota(jnp.int32, full.shape, 0) % rows
            == lax.broadcasted_iota(jnp.int32, full.shape, 1) % rows
        )
        weights[pl.ds(pl.multiple_of(b * tall, tall), tall), :] = jnp.where(same, full, 0.0).astype(BF16)
        return carry

    lax.fori_loop(0, members * rows // tall, expand, 0)
    lax.fori_loop(7, channels, lambda c, carry: (next_in(c), carry)[1], 0)
    own_in.wait()

    high = 256

    def analyse(p, carry):
        for h in range(2):
            c = 2 * p + h
            drain(arrived.at[others, pl.ds(c, 1)], in_recv.at[c])
            total = jnp.zeros((rows, cols), F32)
            for k in range(0, members, step):
                total = total + jnp.sum(arrived[k : k + step, c].astype(F32), axis=0)
            mean = total * (1.0 / members)
            means[h] = mean
            for k in range(0, members, step):
                part = (arrived[k : k + step, c].astype(F32) - mean[None]).astype(BF16)
                perts[k * rows : (k + step) * rows, h * cols : (h + 1) * cols] = part.reshape(step * rows, cols)

        def mix(b, inner):
            at = pl.ds(pl.multiple_of(b * high, high), high)
            shifted = jnp.dot(weights[at, :], perts[...], preferred_element_type=F32)
            for h in range(2):
                part = shifted[:, h * cols : (h + 1) * cols].reshape(high // rows, rows, cols) + means[h][None]
                analysed[pl.ds(b * (high // rows), high // rows), 2 * p + h] = part.astype(BF16)
            return inner

        lax.fori_loop(0, members * rows // high, mix, 0)

        def one(i, inner):
            q = peer(me, n, i)
            pltpu.make_async_remote_copy(
                src_ref=analysed.at[pl.ds(q * per, per), pl.ds(2 * p, 2)],
                dst_ref=out.at[:, pl.ds(2 * p, 2), :, columns(me)],
                send_sem=out_send, recv_sem=out_recv,
                device_id={"mem": q}, device_id_type=MESH,
            ).start()
            return inner

        lax.fori_loop(0, n - 1, one, 0)
        return carry

    lax.fori_loop(0, channels // 2, analyse, 0)
    own_out = pltpu.make_async_copy(analysed.at[mine], out.at[:, :, :, columns(me)], own_sem.at[2])
    own_out.start()

    drain(projected.at[others], proj_send)
    drain(near, gram_send)
    for c in (channels - 2, channels - 1):
        drain(arrived.at[others, pl.ds(c, 1)], in_send.at[c])
    own_out.wait()
    drain(analysed.at[others], out_send)
    drain(analysed.at[others], out_recv)


def shards(state, obs_cell, obs_value, obs_rinv, obs_count, loc_blocks, chan_weight):
    per, channels, rows, width = state.shape
    n = lax.axis_size("mem")
    members, cols = per * n, width // n
    slots = obs_cell.shape[2]
    lanes = 128
    obs_shape = (slots // lanes, lanes)
    whole = pl.BlockSpec(memory_space=pl.ANY)
    scalars = pl.BlockSpec(memory_space=pltpu.SMEM)
    dma = pltpu.SemaphoreType.DMA
    return pl.pallas_call(
        kernel,
        out_shape=jax.ShapeDtypeStruct(state.shape, BF16),
        in_specs=[scalars] * 3 + [whole] * 4,
        out_specs=whole,
        scratch_shapes=[
            pltpu.VMEM(state.shape, BF16),
            pltpu.VMEM(obs_shape, jnp.int32),
            pltpu.VMEM(obs_shape, F32),
            pltpu.VMEM(obs_shape, F32),
            pltpu.VMEM((per, rows, width), BF16),
            pltpu.VMEM((members, rows, cols), BF16),
            pltpu.VMEM((128, rows, cols), F32),
            pltpu.VMEM((members, 128), F32),
            pltpu.VMEM((members, 128), BF16),
            pltpu.VMEM((8, members, 128), BF16),
            pltpu.VMEM((members, channels, rows, cols), BF16),
            pltpu.VMEM((members, members * rows), BF16),
            pltpu.VMEM((members * rows, members * rows), BF16),
            pltpu.VMEM((members * rows, 2 * cols), BF16),
            pltpu.VMEM((2, rows, cols), F32),
            pltpu.VMEM((members, channels, rows, cols), BF16),
            dma((per,)),
            dma((3,)),
            dma((3,)),
            dma, dma, dma, dma,
            dma((channels,)),
            dma((channels,)),
            dma, dma,
        ],
        compiler_params=pltpu.CompilerParams(
            collective_id=0, has_side_effects=True, vmem_limit_bytes=56 * 2**20
        ),
        name="letkf",
    )(
        chan_weight, obs_count, loc_blocks[0],
        state, obs_cell.reshape(obs_shape), obs_value.reshape(obs_shape), obs_rinv.reshape(obs_shape),
    )


def solution(mesh):
    placed = (
        P("mem", None, "lat", None),
        P("lat", "mem", None),
        P("lat", "mem", None),
        P("lat", "mem", None),
        P("lat", "mem"),
        P("lat", "mem", None),
        P(),
    )
    return jax.shard_map(
        shards, mesh=mesh, in_specs=placed, out_specs=P("mem", None, "lat", None), check_vma=False
    )
```

time: 295 us -> 160 us (0.54)
  the two profiles are of different devices: /device:TPU:9 before, /device:TPU:33 now
where the time goes in v1:
time: 160 us
  Pallas kernels  156 us (98%)
  local copies, waits for them, and re-layouts  3.97 us (2%)
    pallas_call x1, Pallas kernels, shards(): pl.pallas_call(kernel, out_shape=jax.ShapeDtypeStruct(state.shape, BF16),...  156 us
    unnamed x1, local copies, waits for them, and re-layouts  3.97 us

profile of v1, /device:TPU:33, one launch (start us, length us, event | category | flops | bytes accessed | tf_op | source)
XLA Modules:
  0.0 160.2 jit_solution(9875918224546744557)
XLA Ops:
  0.7 155.6 %letkf.1 = bf16[4,12,16,2048]{3,2,1,0:T(8,128)(2,1)} custom-call(f32[12]{0:T(128)} %weight.1, s32[1,1]{1,0:T(1,128)S(6)} %copy.9.count, s32[1,9]{1,0:T(1,128)} %bitcast.7, bf16[4,12,16,2048]{3,2,1,0:T(8,128)(2,1)} %x.1, s32[128,128]{1,0:T(8,128)} %bitcast.4, f32[128,128]{1,0:T(8,128)} %bitcast.5, f32[128,128]{1,0:T(8,128)} %bitcast.6), custom_call_target="tpu_custom_call" | custom-call | tf_op jit(solution)/shard_map/letkf/pallas_call | solution.py:311
  156.2 4.0 %copy.10 = bf16[4,12,16,2048]{3,2,1,0:T(8,128)(2,1)} copy(bf16[4,12,16,2048]{3,2,1,0:T(8,128)(2,1)} %letkf.1) | data formatting | bytes 6291456

commit v2 on v1

--- a/solution.py
+++ b/solution.py
@@ -23,12 +23,27 @@
     return ((me // 2 + offset) % (size // 2)) * 2 + (me + flip) % 2
 
 
+def basis(weight):
+    channels = weight.shape[0]
+    big = 2.0**60
+    total = (weight[0] * big) * (weight[0] * big)
+    for c in range(1, channels):
+        total = total + (weight[c] * big) * (weight[c] * big)
+    norm = jnp.sqrt(jnp.full((8, 128), total, F32))
+    some = norm > 0.0
+    inverse = jnp.where(some, 1.0 / jnp.where(some, norm, 1.0), 0.0)
+    first = jnp.where(some, jnp.abs(weight[0]) * big * inverse, 1.0)
+    sign = jnp.where(weight[0] < 0.0, -1.0, 1.0)
+    a, g = jnp.max(first), jnp.max(1.0 / (1.0 + first))
+    return a, jnp.max(inverse) * big * sign, g, jnp.max(norm) * (1.0 / big) * sign
+
+
 def kernel(
     weight, count, loc,
     x, cell, value, rinv,
     out,
-    xv, cellv, valuev, rinvv, proj, projected, table, gram, gram_out, near, arrived, spread, weights, perts, means, analysed,
-    load_sem, obs_sem, own_sem, proj_send, proj_recv, gram_send, gram_recv, in_send, in_recv, out_send, out_recv,
+    xv, cellv, valuev, rinvv, shared, table, gram, gram_out, near, arrived, spread, weights, perts, means, analysed,
+    load_sem, obs_sem, own_sem, gram_send, gram_recv, in_send, in_recv, out_send, out_recv,
 ):
     n = lax.axis_size("mem")
     bands = lax.axis_size("lat")
@@ -66,41 +81,43 @@
         if i != 0:
             pl.semaphore_signal(barrier, inc=1, device_id=neighbour(i, j), device_id_type=MESH)
 
+    a, per_weight, g, to_observed = basis(weight)
     wide = 256
     for m in range(per):
         loads[m].wait()
 
-        def project(b, carry):
+        def first_channel(b, carry):
             at = pl.ds(pl.multiple_of(b * wide, wide), wide)
-            total = xv[m, 0, :, at].astype(F32) * weight[0]
+            x0 = xv[m, 0, :, at].astype(F32)
+            total = x0 * a
             for c in range(1, channels):
-                total = total + xv[m, c, :, at].astype(F32) * weight[c]
-            proj[m, :, at] = total.astype(BF16)
+                total = total + xv[m, c, :, at].astype(F32) * (weight[c] * per_weight)
+            xv[m, 0, :, at] = total.astype(BF16)
+            shared[m, :, at] = total + x0
             return carry
 
-        lax.fori_loop(0, width // wide, project, 0)
+        lax.fori_loop(0, width // wide, first_channel, 0)
+
+    def other_channel(c):
+        factor = weight[c] * per_weight * g
+
+        def one(b, carry):
+            at = pl.ds(pl.multiple_of(b * wide, wide), wide)
+            for m in range(per):
+                xv[m, c, :, at] = (xv[m, c, :, at].astype(F32) - shared[m, :, at] * factor).astype(BF16)
+            return carry
+
+        lax.fori_loop(0, width // wide, one, 0)
 
     pl.semaphore_wait(barrier, n - 1 + 6)
 
     mine = pl.ds(pl.multiple_of(me * per, per), per)
-
-    def send_proj(i, carry):
-        q = peer(me, n, i)
-        pltpu.make_async_remote_copy(
-            src_ref=proj.at[:, :, columns(q)],
-            dst_ref=projected.at[mine],
-            send_sem=proj_send, recv_sem=proj_recv,
-            device_id={"mem": q}, device_id_type=MESH,
-        ).start()
-        return carry
-
-    lax.fori_loop(0, n - 1, send_proj, 0)
 
     def send_in(c):
         def one(i, carry):
             q = peer(me, n, i)
             pltpu.make_async_remote_copy(
-                src_ref=x.at[:, pl.ds(c, 1), :, columns(q)],
+                src_ref=xv.at[:, pl.ds(c, 1), :, columns(q)],
                 dst_ref=arrived.at[mine, pl.ds(c, 1)],
                 send_sem=in_send.at[c], recv_sem=in_recv.at[c],
                 device_id={"mem": q}, device_id_type=MESH,
@@ -115,15 +132,21 @@
     others = pl.ds(0, members - per)
 
     def next_in(c):
-        drain(arrived.at[others, pl.ds(c - 2, 1)], in_send.at[c - 2])
+        drain(arrived.at[others, pl.ds(c - 3, 1)], in_send.at[c - 3])
         send_in(c)
 
-    own_proj = pltpu.make_async_copy(proj.at[:, :, columns(me)], projected.at[mine], own_sem.at[0])
-    own_in = pltpu.make_async_copy(x.at[:, :, :, columns(me)], arrived.at[mine], own_sem.at[1])
-    own_proj.start()
-    own_in.start()
+    def own_in(start, size, i):
+        return pltpu.make_async_copy(
+            xv.at[:, pl.ds(start, size), :, columns(me)], arrived.at[mine, pl.ds(start, size)], own_sem.at[i]
+        )
+
     send_in(0)
-    send_in(1)
+    own_in(0, 1, 0).start()
+    for c in (1, 2):
+        other_channel(c)
+        send_in(c)
+    lax.fori_loop(3, channels, lambda c, carry: (other_channel(c), carry)[1], 0)
+    own_in(1, channels - 1, 1).start()
 
     for_member = lax.broadcasted_iota(jnp.int32, (members, members * rows), 0)
     spread[...] = jnp.where(
@@ -162,27 +185,27 @@
     sums = lax.fori_loop(0, cellv.shape[0] // block, histogram, jnp.zeros((4 * rows, cols), F32))
     cell_rinv = sums[:rows] + sums[rows : 2 * rows]
     cell_held = sums[2 * rows : 3 * rows] + sums[3 * rows :]
-    next_in(2)
-
-    own_proj.wait()
-    drain(projected.at[others], proj_recv)
+    next_in(3)
+
+    own_in(0, 1, 0).wait()
+    drain(arrived.at[others, pl.ds(0, 1)], in_recv.at[0])
     step = 8
     total = jnp.zeros((rows, cols), F32)
     for k in range(0, members, step):
-        total = total + jnp.sum(projected[k : k + step].astype(F32), axis=0)
+        total = total + jnp.sum(arrived[k : k + step, 0].astype(F32), axis=0)
     obs_mean = total * (1.0 / members)
     seen = cell_rinv > 0.0
     root_rinv = jnp.sqrt(cell_rinv)
     inverse = jnp.where(seen, 1.0 / jnp.where(seen, root_rinv, 1.0), 0.0)
+    scale = root_rinv * to_observed
     for k in range(0, members, step):
-        table[k : k + step] = (projected[k : k + step].astype(F32) - obs_mean[None]) * root_rinv[None]
+        table[k : k + step] = (arrived[k : k + step, 0].astype(F32) - obs_mean[None]) * scale[None]
     tail = table.shape[0] - members
     table[members:] = jnp.zeros((tail, rows, cols), F32)
-    table[members] = (cell_held - cell_rinv * obs_mean) * inverse
+    table[members] = (cell_held - cell_rinv * (obs_mean * to_observed)) * inverse
     lines = jnp.concatenate([table[:, r, :].astype(BF16) for r in range(rows)], axis=1)
     gram[...] = lax.dot_general(lines[:members], lines, (((1,), (1,)), ((), ())), preferred_element_type=F32)
     gram_out[...] = gram[...].astype(BF16)
-    next_in(3)
 
     for s, (i, j) in enumerate(neighbours):
         pltpu.make_async_remote_copy(
@@ -245,14 +268,19 @@
 
     lax.fori_loop(0, members * rows // tall, expand, 0)
     lax.fori_loop(7, channels, lambda c, carry: (next_in(c), carry)[1], 0)
-    own_in.wait()
+    own_in(1, channels - 1, 1).wait()
 
     high = 256
 
     def analyse(p, carry):
         for h in range(2):
             c = 2 * p + h
-            drain(arrived.at[others, pl.ds(c, 1)], in_recv.at[c])
+            if h == 0:
+                @pl.when(p > 0)
+                def _():
+                    drain(arrived.at[others, pl.ds(c, 1)], in_recv.at[c])
+            else:
+                drain(arrived.at[others, pl.ds(c, 1)], in_recv.at[c])
             total = jnp.zeros((rows, cols), F32)
             for k in range(0, members, step):
                 total = total + jnp.sum(arrived[k : k + step, c].astype(F32), axis=0)
@@ -289,13 +317,38 @@
     own_out = pltpu.make_async_copy(analysed.at[mine], out.at[:, :, :, columns(me)], own_sem.at[2])
     own_out.start()
 
-    drain(projected.at[others], proj_send)
     drain(near, gram_send)
-    for c in (channels - 2, channels - 1):
+    for c in range(channels - 3, channels):
         drain(arrived.at[others, pl.ds(c, 1)], in_send.at[c])
     own_out.wait()
     drain(analysed.at[others], out_send)
     drain(analysed.at[others], out_recv)
+
+
+def restore(weight, z, out, staged, sem):
+    per, channels, _, width = z.shape
+    a, per_weight, g, _ = basis(weight)
+    wide = 256
+    copies = []
+    for m in range(per):
+
+        def one(b, carry):
+            at = pl.ds(pl.multiple_of(b * wide, wide), wide)
+            z0 = z[m, 0, :, at].astype(F32)
+            rest = z[m, 1, :, at].astype(F32) * (weight[1] * per_weight)
+            for c in range(2, channels):
+                rest = rest + z[m, c, :, at].astype(F32) * (weight[c] * per_weight)
+            staged[m, 0, :, at] = (z0 * a - rest).astype(BF16)
+            shared = z0 - rest * g
+            for c in range(1, channels):
+                staged[m, c, :, at] = (z[m, c, :, at].astype(F32) + shared * (weight[c] * per_weight)).astype(BF16)
+            return carry
+
+        lax.fori_loop(0, width // wide, one, 0)
+        copies.append(pltpu.make_async_copy(staged.at[m], out.at[m], sem.at[m]))
+        copies[-1].start()
+    for copy in copies:
+        copy.wait()
 
 
 def shards(state, obs_cell, obs_value, obs_rinv, obs_count, loc_blocks, chan_weight):
@@ -308,9 +361,9 @@
     whole = pl.BlockSpec(memory_space=pl.ANY)
     scalars = pl.BlockSpec(memory_space=pltpu.SMEM)
     dma = pltpu.SemaphoreType.DMA
-    return pl.pallas_call(
+    analysed = pl.pallas_call(
         kernel,
-        out_shape=jax.ShapeDtypeStruct(state.shape, BF16),
+        out_shape=pltpu.VMEM(state.shape, BF16),
         in_specs=[scalars] * 3 + [whole] * 4,
         out_specs=whole,
         scratch_shapes=[
@@ -318,8 +371,7 @@
             pltpu.VMEM(obs_shape, jnp.int32),
             pltpu.VMEM(obs_shape, F32),
             pltpu.VMEM(obs_shape, F32),
-            pltpu.VMEM((per, rows, width), BF16),
-            pltpu.VMEM((members, rows, cols), BF16),
+            pltpu.VMEM((per, rows, width), F32),
             pltpu.VMEM((128, rows, cols), F32),
             pltpu.VMEM((members, 128), F32),
             pltpu.VMEM((members, 128), BF16),
@@ -333,19 +385,29 @@
             dma((per,)),
             dma((3,)),
             dma((3,)),
-            dma, dma, dma, dma,
+            dma, dma,
             dma((channels,)),
             dma((channels,)),
             dma, dma,
         ],
         compiler_params=pltpu.CompilerParams(
-            collective_id=0, has_side_effects=True, vmem_limit_bytes=56 * 2**20
+            collective_id=0, has_side_effects=True, vmem_limit_bytes=63_800_000
         ),
         name="letkf",
     )(
         chan_weight, obs_count, loc_blocks[0],
         state, obs_cell.reshape(obs_shape), obs_value.reshape(obs_shape), obs_rinv.reshape(obs_shape),
     )
+
+    return pl.pallas_call(
+        restore,
+        out_shape=jax.ShapeDtypeStruct(state.shape, BF16),
+        in_specs=[scalars, pl.BlockSpec(memory_space=pltpu.VMEM)],
+        out_specs=whole,
+        scratch_shapes=[pltpu.VMEM(state.shape, BF16), dma((per,))],
+        compiler_params=pltpu.CompilerParams(vmem_limit_bytes=24 * 2**20),
+        name="restore",
+    )(chan_weight, analysed)
 
 
 def solution(mesh):

time: 160 us -> 154 us (0.963)
  local copies, waits for them, and re-layouts: 3.97 us -> 0.01 us
  Pallas kernels: 156 us -> 153 us
    unnamed x1 -> x2, local copies, waits for them, and re-layouts: 3.97 us -> 0.01 us
    pallas_call x1 -> x2, Pallas kernels: 156 us -> 153 us  [the longest x1 150 us: shards(): pl.pallas_call(kernel, out_shape=pltpu.VMEM(state.shape, BF16), in_specs=...]
where the time goes in v2:
time: 154 us
  Pallas kernels  153 us (99%)
    pallas_call x1, Pallas kernels, shards(): pl.pallas_call(kernel, out_shape=pltpu.VMEM(state.shape, BF16), in_specs=...  150 us

profile of v2, /device:TPU:33, one launch (start us, length us, event | category | flops | bytes accessed | tf_op | source)
XLA Modules:
  0.0 153.6 jit_solution(14506091424147386740)
XLA Ops:
  0.7 0.0 copy-start
  0.7 149.8 %letkf.1.z = bf16[4,12,16,2048]{3,2,1,0:T(8,128)(2,1)S(1)} custom-call(f32[12]{0:T(128)} %weight.3, s32[1,1]{1,0:T(1,128)S(6)} %copy.8.count, s32[1,9]{1,0:T(1,128)} %bitcast.7, bf16[4,12,16,2048]{3,2,1,0:T(8,128)(2,1)} %x.1, s32[128,128]{1,0:T(8,128)} %bitcast.4, f32[128,128]{1,0:T(8,128)} %bitcast.5, f32[128,128]{1,0:T(8,128)} %bitcast.6), custom_call_target="tpu_custom_call" | custom-call | tf_op jit(solution)/shard_map/letkf/pallas_call | solution.py:364
  150.5 0.0 copy-done
  150.5 3.1 %restore.1 = bf16[4,12,16,2048]{3,2,1,0:T(8,128)(2,1)} custom-call(f32[12]{0:T(128)S(1)} %copy-done, bf16[4,12,16,2048]{3,2,1,0:T(8,128)(2,1)S(1)} %letkf.1.z), custom_call_target="tpu_custom_call" | custom-call | tf_op jit(solution)/shard_map/restore/pallas_call | solution.py:402
Async XLA Ops:
  0.7 149.8 %copy-start = (f32[12]{0:T(128)S(1)}, f32[12]{0:T(128)}, u32[]{:S(2)}) copy-start(f32[12]{0:T(128)} %weight.3) | copy-start | bytes 148

commit v3 on v2

--- a/solution.py
+++ b/solution.py
@@ -301,16 +301,22 @@
         lax.fori_loop(0, members * rows // high, mix, 0)
 
         def one(i, inner):
-            q = peer(me, n, i)
-            pltpu.make_async_remote_copy(
-                src_ref=analysed.at[pl.ds(q * per, per), pl.ds(2 * p, 2)],
-                dst_ref=out.at[:, pl.ds(2 * p, 2), :, columns(me)],
-                send_sem=out_send, recv_sem=out_recv,
-                device_id={"mem": q}, device_id_type=MESH,
-            ).start()
+            last = (p == channels // 2 - 1).astype(jnp.int32)
+            fixed = jnp.where(i < 5, i + 1, jnp.where(i == 5, 0, i))
+            q = jnp.where(last == 1, fixed, peer(me, n, jnp.minimum(i, n - 2)))
+
+            @pl.when(jnp.where(last == 1, (q != me).astype(jnp.int32), (i < n - 1).astype(jnp.int32)) == 1)
+            def _():
+                pltpu.make_async_remote_copy(
+                    src_ref=analysed.at[pl.ds(q * per, per), pl.ds(2 * p, 2)],
+                    dst_ref=out.at[:, pl.ds(2 * p, 2), :, columns(me)],
+                    send_sem=out_send, recv_sem=out_recv,
+                    device_id={"mem": q}, device_id_type=MESH,
+                ).start()
+
             return inner
 
-        lax.fori_loop(0, n - 1, one, 0)
+        lax.fori_loop(0, n, one, 0)
         return carry
 
     lax.fori_loop(0, channels // 2, analyse, 0)

time: 154 us -> 151 us (0.981)
  Pallas kernels: 153 us -> 149 us
    pallas_call x1, Pallas kernels: 150 us -> 146 us  [shards(): pl.pallas_call(kernel, out_shape=pltpu.VMEM(state.shape, BF16), in_specs=...]
where the time goes in v3:
time: 151 us; the launch traced here: 150 us
  Pallas kernels  149 us (99%)
    pallas_call x1, Pallas kernels, shards(): pl.pallas_call(kernel, out_shape=pltpu.VMEM(state.shape, BF16), in_specs=...  146 us
    pallas_call x1, Pallas kernels, shards(): pl.pallas_call(restore, out_shape=jax.ShapeDtypeStruct(state.shape, BF16)...  3.07 us

profile of v3, /device:TPU:33, one launch (start us, length us, event | category | flops | bytes accessed | tf_op | source)
XLA Modules:
  0.0 150.0 jit_solution(15656044001569576326)
XLA Ops:
  0.7 0.0 copy-start
  0.7 146.3 %letkf.1.z = bf16[4,12,16,2048]{3,2,1,0:T(8,128)(2,1)S(1)} custom-call(f32[12]{0:T(128)} %weight.3, s32[1,1]{1,0:T(1,128)S(6)} %copy.8.count, s32[1,9]{1,0:T(1,128)} %bitcast.7, bf16[4,12,16,2048]{3,2,1,0:T(8,128)(2,1)} %x.1, s32[128,128]{1,0:T(8,128)} %bitcast.4, f32[128,128]{1,0:T(8,128)} %bitcast.5, f32[128,128]{1,0:T(8,128)} %bitcast.6), custom_call_target="tpu_custom_call" | custom-call | tf_op jit(solution)/shard_map/letkf/pallas_call | solution.py:370
  146.9 0.0 copy-done
  147.0 3.1 %restore.1 = bf16[4,12,16,2048]{3,2,1,0:T(8,128)(2,1)} custom-call(f32[12]{0:T(128)S(1)} %copy-done, bf16[4,12,16,2048]{3,2,1,0:T(8,128)(2,1)S(1)} %letkf.1.z), custom_call_target="tpu_custom_call" | custom-call | tf_op jit(solution)/shard_map/restore/pallas_call | solution.py:408
Async XLA Ops:
  0.7 146.3 %copy-start = (f32[12]{0:T(128)S(1)}, f32[12]{0:T(128)}, u32[]{:S(2)}) copy-start(f32[12]{0:T(128)} %weight.3) | copy-start | bytes 148

commit v4 on v3

--- a/solution.py
+++ b/solution.py
@@ -39,11 +39,10 @@
 
 
 def kernel(
-    weight, count, loc,
-    x, cell, value, rinv,
+    weight_in, count_in, loc_in, x, cell, value, rinv,
     out,
-    xv, cellv, valuev, rinvv, shared, table, gram, gram_out, near, arrived, spread, weights, perts, means, analysed,
-    load_sem, obs_sem, own_sem, gram_send, gram_recv, in_send, in_recv, out_send, out_recv,
+    weight, count, loc, xv, cellv, valuev, rinvv, shared, table, gram, gram_out, near, arrived, spread, weights, perts, means, analysed,
+    scalar_sem, load_sem, obs_sem, own_sem, gram_send, gram_recv, in_send, in_recv, out_send, out_recv,
 ):
     n = lax.axis_size("mem")
     bands = lax.axis_size("lat")
@@ -52,6 +51,31 @@
     members = per * n
     cols = width // n
 
+    def columns(q):
+        return pl.ds(pl.multiple_of(q * cols, cols), cols)
+
+    neighbours = [(i, j) for i in (-1, 0, 1) for j in (-1, 0, 1) if (i, j) != (0, 0)]
+
+    def neighbour(i, j):
+        return {"lat": (band + i + bands) % bands, "mem": (me + j + n) % n}
+
+    barrier = pltpu.get_barrier_semaphore()
+
+    def greet(i, carry):
+        pl.semaphore_signal(barrier, inc=1, device_id={"mem": peer(me, n, i)}, device_id_type=MESH)
+        return carry
+
+    lax.fori_loop(0, n - 1, greet, 0)
+    for i, j in neighbours:
+        if i != 0:
+            pl.semaphore_signal(barrier, inc=1, device_id=neighbour(i, j), device_id_type=MESH)
+
+    scalar_loads = [
+        pltpu.make_async_copy(source, target, scalar_sem.at[i])
+        for i, (source, target) in enumerate(((weight_in, weight), (count_in, count), (loc_in, loc)))
+    ]
+    for load in scalar_loads:
+        load.start()
     loads = [pltpu.make_async_copy(x.at[m], xv.at[m], load_sem.at[m]) for m in range(per)]
     for load in loads:
         load.start()
@@ -62,24 +86,8 @@
     for load in obs_loads:
         load.start()
 
-    def columns(q):
-        return pl.ds(pl.multiple_of(q * cols, cols), cols)
-
-    neighbours = [(i, j) for i in (-1, 0, 1) for j in (-1, 0, 1) if (i, j) != (0, 0)]
-
-    def neighbour(i, j):
-        return {"lat": (band + i + bands) % bands, "mem": (me + j + n) % n}
-
-    barrier = pltpu.get_barrier_semaphore()
-
-    def greet(i, carry):
-        pl.semaphore_signal(barrier, inc=1, device_id={"mem": peer(me, n, i)}, device_id_type=MESH)
-        return carry
-
-    lax.fori_loop(0, n - 1, greet, 0)
-    for i, j in neighbours:
-        if i != 0:
-            pl.semaphore_signal(barrier, inc=1, device_id=neighbour(i, j), device_id_type=MESH)
+    for load in scalar_loads:
+        load.wait()
 
     a, per_weight, g, to_observed = basis(weight)
     wide = 256
@@ -310,7 +318,7 @@
                 pltpu.make_async_remote_copy(
                     src_ref=analysed.at[pl.ds(q * per, per), pl.ds(2 * p, 2)],
                     dst_ref=out.at[:, pl.ds(2 * p, 2), :, columns(me)],
-                    send_sem=out_send, recv_sem=out_recv,
+                    send_sem=out_send, recv_sem=out_recv.at[jnp.where(last == 1, me, n)],
                     device_id={"mem": q}, device_id_type=MESH,
                 ).start()
 
@@ -326,33 +334,56 @@
     drain(near, gram_send)
     for c in range(channels - 3, channels):
         drain(arrived.at[others, pl.ds(c, 1)], in_send.at[c])
+    drain(analysed.at[others, pl.ds(0, channels - 2)], out_recv.at[n])
     own_out.wait()
+
+    def term(m, c, q):
+        return out[m, c, :, columns(q)].astype(F32) * (weight[c] * per_weight)
+
+    def gather(q, carry):
+        for m in range(per):
+            rest = term(m, 1, q)
+            for c in range(2, channels - 2):
+                rest = rest + term(m, c, q)
+            shared[m, :, columns(q)] = rest
+        return carry
+
+    lax.fori_loop(0, n, gather, 0)
+
+    def restore(q):
+        for m in range(per):
+            z0 = out[m, 0, :, columns(q)].astype(F32)
+            rest = shared[m, :, columns(q)] + (term(m, channels - 2, q) + term(m, channels - 1, q))
+            out[m, 0, :, columns(q)] = (z0 * a - rest).astype(BF16)
+            common = z0 - rest * g
+            for c in range(1, channels):
+                kept = out[m, c, :, columns(q)].astype(F32)
+                out[m, c, :, columns(q)] = (kept + common * (weight[c] * per_weight)).astype(BF16)
+
+    restore(me)
+
+    def take(i, carry):
+        q = peer(me, n, i)
+        drain(out.at[:, pl.ds(channels - 2, 2), :, columns(q)], out_recv.at[q])
+        restore(q)
+        return carry
+
+    lax.fori_loop(0, n - 1, take, 0)
     drain(analysed.at[others], out_send)
-    drain(analysed.at[others], out_recv)
-
-
-def restore(weight, z, out, staged, sem):
-    per, channels, _, width = z.shape
-    a, per_weight, g, _ = basis(weight)
-    wide = 256
-    copies = []
-    for m in range(per):
-
-        def one(b, carry):
-            at = pl.ds(pl.multiple_of(b * wide, wide), wide)
-            z0 = z[m, 0, :, at].astype(F32)
-            rest = z[m, 1, :, at].astype(F32) * (weight[1] * per_weight)
-            for c in range(2, channels):
-                rest = rest + z[m, c, :, at].astype(F32) * (weight[c] * per_weight)
-            staged[m, 0, :, at] = (z0 * a - rest).astype(BF16)
-            shared = z0 - rest * g
-            for c in range(1, channels):
-                staged[m, c, :, at] = (z[m, c, :, at].astype(F32) + shared * (weight[c] * per_weight)).astype(BF16)
-            return carry
-
-        lax.fori_loop(0, width // wide, one, 0)
-        copies.append(pltpu.make_async_copy(staged.at[m], out.at[m], sem.at[m]))
-        copies[-1].start()
+
+
+def put(z, out, sem):
+    per, channels, _, _ = z.shape
+    half = channels // 2
+    copies = [
+        pltpu.make_async_copy(
+            z.at[m, pl.ds(h * half, half)], out.at[m, pl.ds(h * half, half)], sem.at[2 * m + h]
+        )
+        for m in range(per)
+        for h in range(2)
+    ]
+    for copy in copies:
+        copy.start()
     for copy in copies:
         copy.wait()
 
@@ -365,14 +396,16 @@
     lanes = 128
     obs_shape = (slots // lanes, lanes)
     whole = pl.BlockSpec(memory_space=pl.ANY)
-    scalars = pl.BlockSpec(memory_space=pltpu.SMEM)
     dma = pltpu.SemaphoreType.DMA
     analysed = pl.pallas_call(
         kernel,
         out_shape=pltpu.VMEM(state.shape, BF16),
-        in_specs=[scalars] * 3 + [whole] * 4,
-        out_specs=whole,
+        in_specs=[whole] * 7,
+        out_specs=pl.BlockSpec(memory_space=pltpu.VMEM),
         scratch_shapes=[
+            pltpu.SMEM(chan_weight.shape, F32),
+            pltpu.SMEM((1, 1), jnp.int32),
+            pltpu.SMEM((1, 9), jnp.int32),
             pltpu.VMEM(state.shape, BF16),
             pltpu.VMEM(obs_shape, jnp.int32),
             pltpu.VMEM(obs_shape, F32),
@@ -388,13 +421,15 @@
             pltpu.VMEM((members * rows, 2 * cols), BF16),
             pltpu.VMEM((2, rows, cols), F32),
             pltpu.VMEM((members, channels, rows, cols), BF16),
+            dma((3,)),
             dma((per,)),
             dma((3,)),
             dma((3,)),
             dma, dma,
             dma((channels,)),
             dma((channels,)),
-            dma, dma,
+            dma,
+            dma((n + 1,)),
         ],
         compiler_params=pltpu.CompilerParams(
             collective_id=0, has_side_effects=True, vmem_limit_bytes=63_800_000
@@ -406,14 +441,14 @@
     )
 
     return pl.pallas_call(
-        restore,
+        put,
         out_shape=jax.ShapeDtypeStruct(state.shape, BF16),
-        in_specs=[scalars, pl.BlockSpec(memory_space=pltpu.VMEM)],
+        in_specs=[pl.BlockSpec(memory_space=pltpu.VMEM)],
         out_specs=whole,
-        scratch_shapes=[pltpu.VMEM(state.shape, BF16), dma((per,))],
+        scratch_shapes=[dma((2 * per,))],
         compiler_params=pltpu.CompilerParams(vmem_limit_bytes=24 * 2**20),
-        name="restore",
-    )(chan_weight, analysed)
+        name="put",
+    )(analysed)
 
 
 def solution(mesh):

time: 151 us -> 151 us (level)
  no operation moved by 1% of the time
where the time goes in v4:
time: 151 us; the launch traced here: 149 us
  Pallas kernels  148 us (98%)
    pallas_call x1, Pallas kernels, shards(): pl.pallas_call(kernel, out_shape=pltpu.VMEM(state.shape, BF16), in_specs=...  147 us

profile of v4, /device:TPU:33, one launch (start us, length us, event | category | flops | bytes accessed | tf_op | source)
XLA Modules:
  0.0 149.1 jit_solution(16041914617796712416)
XLA Ops:
  0.7 146.7 %letkf.1.z = bf16[4,12,16,2048]{3,2,1,0:T(8,128)(2,1)S(1)} custom-call(f32[12]{0:T(128)} %weight_in.1, s32[1,1]{1,0:T(1,128)S(6)} %copy.8.count_in, s32[1,9]{1,0:T(1,128)} %bitcast.7, bf16[4,12,16,2048]{3,2,1,0:T(8,128)(2,1)} %x.1, s32[128,128]{1,0:T(8,128)} %bitcast.4, f32[128,128]{1,0:T(8,128)} %bitcast.5, f32[128,128]{1,0:T(8,128)} %bitcast.6), custom_call_target="tpu_custom_call" | custom-call | tf_op jit(solution)/shard_map/letkf/pallas_call | solution.py:400
  147.4 1.7 %put.1 = bf16[4,12,16,2048]{3,2,1,0:T(8,128)(2,1)} custom-call(bf16[4,12,16,2048]{3,2,1,0:T(8,128)(2,1)S(1)} %letkf.1.z), custom_call_target="tpu_custom_call" | custom-call | tf_op jit(solution)/shard_map/put/pallas_call | solution.py:443

commit v5 on v4

--- a/solution.py
+++ b/solution.py
@@ -310,7 +310,7 @@
 
         def one(i, inner):
             last = (p == channels // 2 - 1).astype(jnp.int32)
-            fixed = jnp.where(i < 5, i + 1, jnp.where(i == 5, 0, i))
+            fixed = jnp.where(i < 4, i + 1, jnp.where(i == 4, 0, i))
             q = jnp.where(last == 1, fixed, peer(me, n, jnp.minimum(i, n - 2)))
 
             @pl.when(jnp.where(last == 1, (q != me).astype(jnp.int32), (i < n - 1).astype(jnp.int32)) == 1)
@@ -363,7 +363,7 @@
     restore(me)
 
     def take(i, carry):
-        q = peer(me, n, i)
+        q = (me + i + 1) % n
         drain(out.at[:, pl.ds(channels - 2, 2), :, columns(q)], out_recv.at[q])
         restore(q)
         return carry

time: 151 us -> 151 us (level)
  no operation moved by 1% of the time
where the time goes in v5:
time: 151 us; the launch traced here: 149 us
  Pallas kernels  148 us (98%)
    pallas_call x1, Pallas kernels, shards(): pl.pallas_call(kernel, out_shape=pltpu.VMEM(state.shape, BF16), in_specs=...  146 us

profile of v5, /device:TPU:33, one launch (start us, length us, event | category | flops | bytes accessed | tf_op | source)
XLA Modules:
  0.0 148.8 jit_solution(13377568477616118365)
XLA Ops:
  0.7 146.4 %letkf.1.z = bf16[4,12,16,2048]{3,2,1,0:T(8,128)(2,1)S(1)} custom-call(f32[12]{0:T(128)} %weight_in.1, s32[1,1]{1,0:T(1,128)S(6)} %copy.8.count_in, s32[1,9]{1,0:T(1,128)} %bitcast.7, bf16[4,12,16,2048]{3,2,1,0:T(8,128)(2,1)} %x.1, s32[128,128]{1,0:T(8,128)} %bitcast.4, f32[128,128]{1,0:T(8,128)} %bitcast.5, f32[128,128]{1,0:T(8,128)} %bitcast.6), custom_call_target="tpu_custom_call" | custom-call | tf_op jit(solution)/shard_map/letkf/pallas_call | solution.py:400
  147.1 1.7 %put.1 = bf16[4,12,16,2048]{3,2,1,0:T(8,128)(2,1)} custom-call(bf16[4,12,16,2048]{3,2,1,0:T(8,128)(2,1)S(1)} %letkf.1.z), custom_call_target="tpu_custom_call" | custom-call | tf_op jit(solution)/shard_map/put/pallas_call | solution.py:443
